TPU v7x, 512 devices: a whole 4x8x8 slice. The times are simulated.
512 devices in a mesh: dp: 32 (over y_lo, z), fsdp: 16 (over x, y_hi, core).
Axes of the slice: x: 4, y: 8 (y_hi: 2, y_lo: 4; y = y_hi * 4 + y_lo), z: 8, core: 2. Of those that a mesh axis runs over, the one named last changes fastest.
Arguments:
- tokens: bfloat16 [65536, 2048], P(('dp', 'fsdp')), may hold values from -6 to 6
- upstream: bfloat16 [65536, 512], P(('dp', 'fsdp')), may hold values from -6 to 6
- value_weight: bfloat16 [2048, 512], P('fsdp'), may hold values from -0.125 to 0.125
- forget_label: int32 [32], P('dp'), may hold values 0 or 1
- copy_index: int32 [32], P('dp'), may hold values from 0 to 1, as said below
- adv_rate: float32 [2], replicated, may hold values from 0.5 to 2
Outputs:
- meta_grad: float32 [2048, 512], P('fsdp')
Inputs may be any that keep to these rules, and one draw needn't show every extreme that they name: `copy_index`: each of the 2 copies is named by exactly 16 sequences.
All inputs are finite; a program needn't handle non-finite values. No bound on the sum of `forget_label` on one device may be relied on, other than what follows from the above.
Results may differ from a plain program's by a relative error of at most 0.0056.
Values may be sent and summed in bfloat16 or wider, within the bound.
A program may use at most 64 MiB of HBM per device.

v0:
```python
import jax
import jax.numpy as jnp
from jax import lax
from jax.sharding import PartitionSpec as P


def first_slope(value):
    sig = jax.nn.sigmoid(value)
    return sig * (1.0 + value * (1.0 - sig))


def second_slope(value):
    sig = jax.nn.sigmoid(value)
    return sig * (1.0 - sig) * (2.0 + value * (1.0 - 2.0 * sig))


def local(tokens, upstream, value_weight, forget_label, copy_index, adv_rate):
    groups = lax.axis_size("fsdp")
    seq_count = lax.axis_size("dp")
    seq_length = tokens.shape[0] * groups
    forget = forget_label[0].astype(jnp.float32)
    onehot = (jnp.arange(adv_rate.shape[0], dtype=jnp.int32) == copy_index[0]).astype(jnp.float32)
    own_rate = jnp.sum(onehot * adv_rate)
    upward = upstream.astype(jnp.float32)

    def project(piece):
        return jnp.dot(tokens, piece, preferred_element_type=jnp.float32)

    primal = project(lax.all_gather(value_weight, "fsdp", axis=0, tiled=True))
    columns = lax.all_to_all(tokens, "fsdp", split_axis=1, concat_axis=0, tiled=True)

    def contract(piece):
        return lax.dot_general(
            columns, piece, (((0,), (0,)), ((), ())), preferred_element_type=jnp.float32
        )

    delta_adv = (forget * upward * first_slope(primal) / seq_length).astype(jnp.bfloat16)
    grad_local = lax.psum_scatter(
        lax.dot_general(
            tokens, delta_adv, (((0,), (0,)), ((), ())), preferred_element_type=jnp.float32
        ),
        "fsdp",
        scatter_dimension=0,
        tiled=True,
    )
    stacked = lax.psum(onehot[:, None, None] * grad_local[None], "dp")
    grad_own = jnp.sum(onehot[:, None, None] * stacked, axis=0)
    attacked = (value_weight.astype(jnp.float32) - own_rate * grad_own).astype(jnp.bfloat16)
    altered = project(lax.all_gather(attacked, "fsdp", axis=0, tiled=True))
    delta_out = ((1.0 - 2.0 * forget) * upward * first_slope(altered) / seq_length).astype(
        jnp.bfloat16
    )
    outer_local = contract(lax.all_gather(delta_out, "fsdp", axis=0, tiled=True))
    outer_all = lax.psum(onehot[:, None, None] * outer_local[None], "dp")
    tangent = jnp.sum(onehot[:, None, None] * outer_all, axis=0).astype(jnp.bfloat16)
    forward_tangent = project(lax.all_gather(tangent, "fsdp", axis=0, tiled=True))
    delta_curv = (forget * upward * second_slope(primal) * forward_tangent / seq_length).astype(
        jnp.bfloat16
    )
    curv_local = contract(lax.all_gather(delta_curv, "fsdp", axis=0, tiled=True))
    curv_sum = lax.psum(own_rate * curv_local, "dp")
    scale = (float(seq_length) / float(seq_count)) ** 0.5
    return scale * (jnp.sum(outer_all, axis=0) - curv_sum)


def solution(mesh):
    in_specs = (
        P(("dp", "fsdp"), None),
        P(("dp", "fsdp"), None),
        P("fsdp", None),
        P("dp"),
        P("dp"),
        P(),
    )
    out_specs = P("fsdp", None)
    return jax.shard_map(local, mesh=mesh, in_specs=in_specs, out_specs=out_specs, check_vma=False)
```

profile of v0, /device:TPU:2, one launch (start us, length us, event | category | flops | bytes accessed | tf_op | source)
XLA Modules:
  0.0 1404.9 jit_solution(12837787341775304741)
XLA Ops:
  6.5 0.0 all-gather.6.cloned.1.call-start
  6.5 0.7 all-gather.6.cloned.1.call-update
  7.3 0.0 reduce-scatter.2.cloned.1.call-start
  8.0 71.3 %all-gather.6.cloned.1.call-done = bf16[2048,512]{1,0:T(8,128)(2,1)} async-done(((bf16[128,512]{1,0:T(8,128)(2,1)}), bf16[2048,512]{1,0:T(8,128)(2,1)}) %all-gather.6.cloned.1.call-update) | async-done | bytes 2097168 | tf_op jit(solution)/shard_map/all_gather | solution.py:29
  79.3 2.2 fusion.21
  81.5 2.7 convolution_bitcast_fusion
  84.2 0.0 reduce-scatter.2.cloned.1.call-update
  84.3 0.0 copy-start.1
  84.3 0.0 all-reduce.4.cloned.1.call-start
  85.0 108.9 %reduce-scatter.2.cloned.1.call-done = f32[128,512]{0,1:T(8,128)} async-done(((f32[2048,512]{0,1:T(8,128)}), f32[128,512]{0,1:T(8,128)}) %reduce-scatter.2.cloned.1.call-update) | async-done | bytes 262160 | tf_op jit(solution)/shard_map/reduce_scatter | solution.py:38
  193.9 1.1 copy.20
  195.0 0.9 broadcast_multiply_fusion.1
  195.9 0.0 all-reduce.4.cloned.1.call-update
  195.9 0.0 all-gather.8.cloned.1.call-start
  196.0 0.7 fusion.18
  196.7 309.2 %all-reduce.4.cloned.1.call-done = f32[2,128,512]{2,1,0:T(8,128)} async-done(((f32[2,128,512]{2,1,0:T(8,128)}), f32[2,128,512]{2,1,0:T(8,128)}) %all-reduce.4.cloned.1.call-update) | async-done | bytes 524304 | tf_op jit(solution)/shard_map/psum | solution.py:46
  505.9 1.2 multiply_reduce_fusion.1
  507.1 1.3 subtract_convert_fusion
  508.4 0.0 all-gather.8.cloned.1.call-update
  508.4 0.0 all-gather.10.cloned.1.call-start
  508.5 59.6 %all-gather.8.cloned.1.call-done = bf16[2048,512]{1,0:T(8,128)(2,1)} async-done(((bf16[128,512]{1,0:T(8,128)(2,1)}), bf16[2048,512]{1,0:T(8,128)(2,1)}) %all-gather.8.cloned.1.call-update) | async-done | bytes 2097168 | tf_op jit(solution)/shard_map/all_gather | solution.py:49
  568.0 2.8 fusion.10
  570.8 0.0 all-gather.10.cloned.1.call-update
  570.8 0.0 all-reduce.6.cloned.1.call-start
  570.9 0.3 copy.22
  571.1 21.9 %all_to_all.19 = bf16[128,16,128]{0,2,1:T(8,128)(2,1)S(1)} all-to-all(bf16[128,16,128]{0,2,1:T(8,128)(2,1)S(1)} %bitcast.39), channel_id=1, replica_groups=mesh['dp'=32,'fsdp'=16] {'fsdp'}, dimensions={1} | all-to-all | bytes 1048576 | tf_op jit(solution)/shard_map/all_to_all | solution.py:30
  593.0 0.3 copy.23
  593.3 46.8 %all-gather.10.cloned.1.call-done = bf16[2048,512]{1,0:T(8,128)(2,1)} async-done(((bf16[128,512]{1,0:T(8,128)(2,1)}), bf16[2048,512]{1,0:T(8,128)(2,1)}) %all-gather.10.cloned.1.call-update) | async-done | bytes 2097168 | tf_op jit(solution)/shard_map/all_gather | solution.py:53
  640.1 2.3 convolution_bitcast_fusion.3
  642.5 0.1 copy.24
  642.6 0.9 broadcast_multiply_fusion
  643.5 0.0 all-reduce.6.cloned.1.call-update
  643.6 0.0 all-gather.12.cloned.1.call-start
  643.6 310.1 %all-reduce.6.cloned.1.call-done = f32[2,128,512]{2,1,0:T(8,128)} async-done(((f32[2,128,512]{2,1,0:T(8,128)}), f32[2,128,512]{2,1,0:T(8,128)}) %all-reduce.6.cloned.1.call-update) | async-done | bytes 524304 | tf_op jit(solution)/shard_map/psum | solution.py:54
  953.7 1.9 multiply_reduce_fusion
  955.6 0.0 all-gather.12.cloned.1.call-update
  955.6 0.0 all-gather.14.cloned.1.call-start
  955.6 60.4 %all-gather.12.cloned.1.call-done = bf16[2048,512]{1,0:T(8,128)(2,1)} async-done(((bf16[128,512]{1,0:T(8,128)(2,1)}), bf16[2048,512]{1,0:T(8,128)(2,1)}) %all-gather.12.cloned.1.call-update) | async-done | bytes 2097168 | tf_op jit(solution)/shard_map/all_gather | solution.py:56
  1016.0 2.7 fusion.3
  1018.7 0.0 all-gather.14.cloned.1.call-update
  1018.8 0.0 all-reduce.8.cloned.1.call-start
  1018.8 64.4 %all-gather.14.cloned.1.call-done = bf16[2048,512]{1,0:T(8,128)(2,1)} async-done(((bf16[128,512]{1,0:T(8,128)(2,1)}), bf16[2048,512]{1,0:T(8,128)(2,1)}) %all-gather.14.cloned.1.call-update) | async-done | bytes 2097168 | tf_op jit(solution)/shard_map/all_gather | solution.py:60
  1083.2 3.7 fusion.2
  1086.8 0.0 all-reduce.8.cloned.1.call-update
  1086.9 0.1 copy.26
  1087.0 309.6 %all-reduce.8.cloned.1.call-done = f32[128,512]{0,1:T(8,128)} async-done(((f32[128,512]{0,1:T(8,128)}), f32[128,512]{0,1:T(8,128)}) %all-reduce.8.cloned.1.call-update) | async-done | bytes 262160 | tf_op jit(solution)/shard_map/psum | solution.py:61
  1396.5 1.0 subtract_multiply_fusion.2
  1397.5 0.8 copy.27
  (8 shorter events, 0.0 us)
Async XLA Ops:
  6.5 75.0 %copy-start = (bf16[128,2048]{1,0:T(8,128)(2,1)S(1)}, bf16[128,2048]{1,0:T(8,128)(2,1)}, u32[]{:S(2)}) copy-start(bf16[128,2048]{1,0:T(8,128)(2,1)} %param.6) | copy-start | bytes 1572868
  6.5 75.0 %copy-start.2 = (bf16[128,512]{1,0:T(8,128)(2,1)S(1)}, bf16[128,512]{1,0:T(8,128)(2,1)}, u32[]{:S(2)}) copy-start(bf16[128,512]{1,0:T(8,128)(2,1)} %param.7) | copy-start | bytes 393220
  6.5 72.8 %all-gather.6.cloned.1.call-start = ((), (), s32[]{:S(2)}) async-start(), calls=%async_computation.2 | async-start | bytes 2228224 | tf_op jit(solution)/shard_map/all_gather | solution.py:29
  7.3 186.6 %reduce-scatter.2.cloned.1.call-start = ((), (), s32[]{:S(2)}) async-start(), calls=%async_computation.3 | async-start | bytes 4456448 | tf_op jit(solution)/shard_map/reduce_scatter | solution.py:38
  84.2 111.8 %copy-start.3 = (f32[2]{0:T(128)S(1)}, f32[2]{0:T(128)}, u32[]{:S(2)}) copy-start(f32[2]{0:T(128)} %param.11) | copy-start | bytes 28
  84.3 422.8 %copy-start.1 = (bf16[128,512]{1,0:T(8,128)(2,1)S(1)}, bf16[128,512]{1,0:T(8,128)(2,1)}, u32[]{:S(2)}) copy-start(bf16[128,512]{1,0:T(8,128)(2,1)} %param.8) | copy-start | bytes 393220
  84.3 421.6 %all-reduce.4.cloned.1.call-start = ((), (), s32[]{:S(2)}) async-start(), calls=%async_computation.4 | async-start | bytes 1048576 | tf_op jit(solution)/shard_map/psum | solution.py:46
  195.9 372.1 %all-gather.8.cloned.1.call-start = ((), (), s32[]{:S(2)}) async-start(), calls=%async_computation.5 | async-start | bytes 2228224 | tf_op jit(solution)/shard_map/all_gather | solution.py:49
  508.4 131.7 %all-gather.10.cloned.1.call-start = ((), (), s32[]{:S(2)}) async-start(), calls=%async_computation.6 | async-start | bytes 2228224 | tf_op jit(solution)/shard_map/all_gather | solution.py:53
  570.8 382.9 %all-reduce.6.cloned.1.call-start = ((), (), s32[]{:S(2)}) async-start(), calls=%async_computation.7 | async-start | bytes 1048576 | tf_op jit(solution)/shard_map/psum | solution.py:54
  643.6 372.5 %all-gather.12.cloned.1.call-start = ((), (), s32[]{:S(2)}) async-start(), calls=%async_computation.8 | async-start | bytes 2228224 | tf_op jit(solution)/shard_map/all_gather | solution.py:56
  955.6 127.6 %all-gather.14.cloned.1.call-start = ((), (), s32[]{:S(2)}) async-start(), calls=%async_computation.9 | async-start | bytes 2228224 | tf_op jit(solution)/shard_map/all_gather | solution.py:60
  1018.8 377.8 %all-reduce.8.cloned.1.call-start = ((), (), s32[]{:S(2)}) async-start(), calls=%async_computation.10 | async-start | bytes 524288 | tf_op jit(solution)/shard_map/psum | solution.py:61
Sparse Core Ops, SparseCore 0:
  10.6 68.6 all-gather.5
  84.4 109.4 reduce-scatter.1
  196.8 309.0 all-reduce.3
  509.0 58.9 all-gather.7
  571.1 68.9 all-gather.9
  643.7 309.9 all-reduce.5
  957.0 58.9 all-gather.11
  1019.3 63.8 all-gather.13
  1087.0 309.5 all-reduce.7
where the time goes:
time: 1410 us; the launch traced here: 1400 us
  waiting for transfers between devices  1340 us (95%)
  blocking collectives  21.9 us (2%)
  matrix products  16.4 us (1%)
  between operations  14.6 us (1%)
    psum x1, waiting for transfers between devices, local(): outer_all = lax.psum(onehot[:, None, None] * outer_local[None], 'dp')  310 us
    psum x1, waiting for transfers between devices, local(): curv_sum = lax.psum(own_rate * curv_local, 'dp')  310 us
    psum x1, waiting for transfers between devices, local(): stacked = lax.psum(onehot[:, None, None] * grad_local[None], 'dp')  309 us
    reduce_scatter x1, waiting for transfers between devices, local(): lax.psum_scatter(lax.dot_general(tokens, delta_adv, (((0,), (0,)), ((), (...  109 us
    all_gather x1, waiting for transfers between devices, local(): primal = project(lax.all_gather(value_weight, 'fsdp', axis=0, tiled=True))  71.3 us
    all_gather x1, waiting for transfers between devices, local(): lax.all_gather(delta_curv, 'fsdp', axis=0, tiled=True)  64.4 us
    all_gather x1, waiting for transfers between devices, local(): lax.all_gather(tangent, 'fsdp', axis=0, tiled=True)  60.4 us
    all_gather x1, waiting for transfers between devices, local(): altered = project(lax.all_gather(attacked, 'fsdp', axis=0, tiled=True))  59.6 us
  transfers between devices with their start and end apart: 9, of which 9 were waited for; matrix products, arithmetic and copies ran while one was open for 0% of the time, Pallas kernels for 0%

commit v1 on v0

--- a/solution.py
+++ b/solution.py
@@ -2,6 +2,7 @@
 import jax.numpy as jnp
 from jax import lax
 from jax.sharding import PartitionSpec as P
+from jax.lax import all_gather
 
 
 def first_slope(value):
@@ -58,7 +59,8 @@
         jnp.bfloat16
     )
     curv_local = contract(lax.all_gather(delta_curv, "fsdp", axis=0, tiled=True))
-    curv_sum = lax.psum(own_rate * curv_local, "dp")
+    x_local = own_rate * curv_local
+    curv_sum = all_gather(x_local, "dp").sum(axis=0)
     scale = (float(seq_length) / float(seq_count)) ** 0.5
     return scale * (jnp.sum(outer_all, axis=0) - curv_sum)
 

time: 1410 us -> 1270 us (0.901)
  the two profiles are of different devices: /device:TPU:2 before, /device:TPU:14 now
where the time goes in v1:
time: 1270 us
  waiting for transfers between devices  1200 us (94%)
  blocking collectives  23.3 us (2%)
  matrix products  16.4 us (1%)
  between operations  14.6 us (1%)
    psum x1, waiting for transfers between devices, local(): outer_all = lax.psum(onehot[:, None, None] * outer_local[None], 'dp')  299 us
    psum x1, waiting for transfers between devices, local(): stacked = lax.psum(onehot[:, None, None] * grad_local[None], 'dp')  299 us
    all_gather x1, waiting for transfers between devices, local(): curv_sum = all_gather(x_local, 'dp').sum(axis=0)  170 us
    reduce_scatter x1, waiting for transfers between devices, local(): lax.psum_scatter(lax.dot_general(tokens, delta_adv, (((0,), (0,)), ((), (...  108 us
    all_gather x1, waiting for transfers between devices, local(): primal = project(lax.all_gather(value_weight, 'fsdp', axis=0, tiled=True))  73.9 us
    all_gather x1, waiting for transfers between devices, local(): lax.all_gather(tangent, 'fsdp', axis=0, tiled=True)  71.8 us
    all_gather x1, waiting for transfers between devices, local(): altered = project(lax.all_gather(attacked, 'fsdp', axis=0, tiled=True))  71 us
    all_gather x1, waiting for transfers between devices, local(): lax.all_gather(delta_curv, 'fsdp', axis=0, tiled=True)  64.4 us
  transfers between devices with their start and end apart: 9, of which 9 were waited for; matrix products, arithmetic and copies ran while one was open for 0% of the time, Pallas kernels for 0%

profile of v1, /device:TPU:14, one launch (start us, length us, event | category | flops | bytes accessed | tf_op | source)
XLA Modules:
  0.0 1273.8 jit_solution(1559684664706206320)
XLA Ops:
  6.5 0.7 all-gather.8.cloned.1.call-update
  7.3 0.0 reduce-scatter.2.cloned.1.call-start
  8.0 73.9 %all-gather.8.cloned.1.call-done = bf16[2048,512]{1,0:T(8,128)(2,1)} async-done(((bf16[128,512]{1,0:T(8,128)(2,1)}), bf16[2048,512]{1,0:T(8,128)(2,1)}) %all-gather.8.cloned.1.call-update) | async-done | bytes 2097168 | tf_op jit(solution)/shard_map/all_gather | solution.py:30
  81.8 2.2 fusion.21
  84.1 2.7 convolution_bitcast_fusion
  86.8 0.0 reduce-scatter.2.cloned.1.call-update
  86.8 0.0 copy-start.1
  86.8 0.0 all-reduce.3.cloned.1.call-start
  87.6 108.0 %reduce-scatter.2.cloned.1.call-done = f32[128,512]{0,1:T(8,128)} async-done(((f32[2048,512]{0,1:T(8,128)}), f32[128,512]{0,1:T(8,128)}) %reduce-scatter.2.cloned.1.call-update) | async-done | bytes 262160 | tf_op jit(solution)/shard_map/reduce_scatter | solution.py:39
  195.6 1.1 copy.24
  196.7 0.9 broadcast_multiply_fusion.1
  197.6 0.0 all-reduce.3.cloned.1.call-update
  197.6 0.0 all-gather.10.cloned.1.call-start
  197.7 0.7 fusion.18
  198.3 298.6 %all-reduce.3.cloned.1.call-done = f32[2,128,512]{2,1,0:T(8,128)} async-done(((f32[2,128,512]{2,1,0:T(8,128)}), f32[2,128,512]{2,1,0:T(8,128)}) %all-reduce.3.cloned.1.call-update) | async-done | bytes 524304 | tf_op jit(solution)/shard_map/psum | solution.py:47
  497.0 1.2 multiply_reduce_fusion.1
  498.2 1.3 subtract_convert_fusion
  499.5 0.0 all-gather.10.cloned.1.call-update
  499.5 0.0 all-gather.12.cloned.1.call-start
  499.6 71.0 %all-gather.10.cloned.1.call-done = bf16[2048,512]{1,0:T(8,128)(2,1)} async-done(((bf16[128,512]{1,0:T(8,128)(2,1)}), bf16[2048,512]{1,0:T(8,128)(2,1)}) %all-gather.10.cloned.1.call-update) | async-done | bytes 2097168 | tf_op jit(solution)/shard_map/all_gather | solution.py:50
  570.6 2.8 fusion.10
  573.3 0.0 all-gather.12.cloned.1.call-update
  573.4 0.0 all-reduce.5.cloned.1.call-start
  573.4 0.3 copy.26
  573.7 23.3 %all_to_all.19 = bf16[128,16,128]{0,2,1:T(8,128)(2,1)S(1)} all-to-all(bf16[128,16,128]{0,2,1:T(8,128)(2,1)S(1)} %bitcast.45), channel_id=1, replica_groups=mesh['dp'=32,'fsdp'=16] {'fsdp'}, dimensions={1} | all-to-all | bytes 1048576 | tf_op jit(solution)/shard_map/all_to_all | solution.py:31
  597.0 0.3 copy.27
  597.3 45.4 %all-gather.12.cloned.1.call-done = bf16[2048,512]{1,0:T(8,128)(2,1)} async-done(((bf16[128,512]{1,0:T(8,128)(2,1)}), bf16[2048,512]{1,0:T(8,128)(2,1)}) %all-gather.12.cloned.1.call-update) | async-done | bytes 2097168 | tf_op jit(solution)/shard_map/all_gather | solution.py:54
  642.7 2.3 convolution_bitcast_fusion.3
  645.0 0.1 copy.28
  645.1 0.9 broadcast_multiply_fusion
  646.1 0.0 all-reduce.5.cloned.1.call-update
  646.1 0.0 all-gather.14.cloned.1.call-start
  646.1 298.7 %all-reduce.5.cloned.1.call-done = f32[2,128,512]{2,1,0:T(8,128)} async-done(((f32[2,128,512]{2,1,0:T(8,128)}), f32[2,128,512]{2,1,0:T(8,128)}) %all-reduce.5.cloned.1.call-update) | async-done | bytes 524304 | tf_op jit(solution)/shard_map/psum | solution.py:55
  944.8 1.9 multiply_reduce_fusion
  946.7 0.0 all-gather.14.cloned.1.call-update
  946.7 0.0 all-gather.16.cloned.1.call-start
  946.7 71.8 %all-gather.14.cloned.1.call-done = bf16[2048,512]{1,0:T(8,128)(2,1)} async-done(((bf16[128,512]{1,0:T(8,128)(2,1)}), bf16[2048,512]{1,0:T(8,128)(2,1)}) %all-gather.14.cloned.1.call-update) | async-done | bytes 2097168 | tf_op jit(solution)/shard_map/all_gather | solution.py:57
  1018.6 2.7 fusion.3
  1021.3 0.0 all-gather.16.cloned.1.call-update
  1021.3 0.0 all-gather.18.cloned.1.call-start
  1021.3 64.4 %all-gather.16.cloned.1.call-done = bf16[2048,512]{1,0:T(8,128)(2,1)} async-done(((bf16[128,512]{1,0:T(8,128)(2,1)}), bf16[2048,512]{1,0:T(8,128)(2,1)}) %all-gather.16.cloned.1.call-update) | async-done | bytes 2097168 | tf_op jit(solution)/shard_map/all_gather | solution.py:61
  1085.7 3.7 fusion.2
  1089.4 0.0 all-gather.18.cloned.1.call-update
  1089.4 170.2 %all-gather.18.cloned.1.call-done = f32[4096,512]{0,1:T(8,128)} async-done(((f32[128,512]{0,1:T(8,128)}), f32[4096,512]{0,1:T(8,128)}) %all-gather.18.cloned.1.call-update) | async-done | bytes 8388624 | tf_op jit(solution)/shard_map/all_gather | solution.py:63
  1259.6 5.2 copy.33
  1264.8 1.6 bitcast_reduce_fusion
  1266.4 0.1 copy.30
  1266.5 0.7 subtract_multiply_fusion.2
  (9 shorter events, 0.0 us)
Async XLA Ops:
  6.5 77.5 %copy-start = (bf16[128,2048]{1,0:T(8,128)(2,1)S(1)}, bf16[128,2048]{1,0:T(8,128)(2,1)}, u32[]{:S(2)}) copy-start(bf16[128,2048]{1,0:T(8,128)(2,1)} %param.6) | copy-start | bytes 1572868
  6.5 77.5 %copy-start.2 = (bf16[128,512]{1,0:T(8,128)(2,1)S(1)}, bf16[128,512]{1,0:T(8,128)(2,1)}, u32[]{:S(2)}) copy-start(bf16[128,512]{1,0:T(8,128)(2,1)} %param.7) | copy-start | bytes 393220
  6.5 75.3 %all-gather.8.cloned.1.call-start = ((), (), s32[]{:S(2)}) async-start(), calls=%async_computation.2 | async-start | bytes 2228224 | tf_op jit(solution)/shard_map/all_gather | solution.py:30
  7.3 188.3 %reduce-scatter.2.cloned.1.call-start = ((), (), s32[]{:S(2)}) async-start(), calls=%async_computation.3 | async-start | bytes 4456448 | tf_op jit(solution)/shard_map/reduce_scatter | solution.py:39
  86.8 110.9 %copy-start.3 = (f32[2]{0:T(128)S(1)}, f32[2]{0:T(128)}, u32[]{:S(2)}) copy-start(f32[2]{0:T(128)} %param.11) | copy-start | bytes 28
  86.8 411.3 %copy-start.1 = (bf16[128,512]{1,0:T(8,128)(2,1)S(1)}, bf16[128,512]{1,0:T(8,128)(2,1)}, u32[]{:S(2)}) copy-start(bf16[128,512]{1,0:T(8,128)(2,1)} %param.8) | copy-start | bytes 393220
  86.8 410.1 %all-reduce.3.cloned.1.call-start = ((), (), s32[]{:S(2)}) async-start(), calls=%async_computation.4 | async-start | bytes 1048576 | tf_op jit(solution)/shard_map/psum | solution.py:47
  197.6 372.9 %all-gather.10.cloned.1.call-start = ((), (), s32[]{:S(2)}) async-start(), calls=%async_computation.5 | async-start | bytes 2228224 | tf_op jit(solution)/shard_map/all_gather | solution.py:50
  499.5 143.2 %all-gather.12.cloned.1.call-start = ((), (), s32[]{:S(2)}) async-start(), calls=%async_computation.6 | async-start | bytes 2228224 | tf_op jit(solution)/shard_map/all_gather | solution.py:54
  573.4 371.5 %all-reduce.5.cloned.1.call-start = ((), (), s32[]{:S(2)}) async-start(), calls=%async_computation.7 | async-start | bytes 1048576 | tf_op jit(solution)/shard_map/psum | solution.py:55
  646.1 372.5 %all-gather.14.cloned.1.call-start = ((), (), s32[]{:S(2)}) async-start(), calls=%async_computation.8 | async-start | bytes 2228224 | tf_op jit(solution)/shard_map/all_gather | solution.py:57
  946.7 139.0 %all-gather.16.cloned.1.call-start = ((), (), s32[]{:S(2)}) async-start(), calls=%async_computation.9 | async-start | bytes 2228224 | tf_op jit(solution)/shard_map/all_gather | solution.py:61
  1021.3 238.3 %all-gather.18.cloned.1.call-start = ((), (), s32[]{:S(2)}) async-start(), calls=%async_computation.10 | async-start | bytes 8650752 | tf_op jit(solution)/shard_map/all_gather | solution.py:63
Sparse Core Ops, SparseCore 0:
  10.6 71.1 all-gather.7
  86.9 108.5 reduce-scatter.1
  198.5 298.4 all-reduce.2
  500.1 70.4 all-gather.9
  573.7 68.9 all-gather.11
  646.2 298.5 all-reduce.4
  948.1 70.4 all-gather.13
  1021.8 63.8 all-gather.15
  1089.5 170.0 all-gather.17
